TPU v7x, 32 devices: a whole 2x2x4 slice. The times are simulated.
32 devices in a mesh: dp: 8 (over z, y), tensor: 4 (over x, core).
Axes of the slice: x: 2, y: 2, z: 4, core: 2. Of those that a mesh axis runs over, the one named last changes fastest.
Arguments:
- tokens: bfloat16 [24, 736, 768], P('dp', None, 'tensor'), may hold values from -6 to 6
- horizon: int32 [24], P('dp'), may hold values from 4 to 30, as said below
- attn_gain: float32 [768], replicated, may hold values from 0.5 to 1.5
- attn_shift: float32 [768], replicated, may hold values from -1.5 to 1.5
- query_weight: bfloat16 [768, 768], P(None, 'tensor'), may hold values from -0.21875 to 0.21875
- key_weight: bfloat16 [768, 768], P(None, 'tensor'), may hold values from -0.21875 to 0.21875
- value_weight: bfloat16 [768, 768], P(None, 'tensor'), may hold values from -0.21875 to 0.21875
- query_bias: float32 [768], P('tensor'), may hold values from -2.5 to 2.5
- value_bias: float32 [768], P('tensor'), may hold values from -2.5 to 2.5
- output_weight: bfloat16 [768, 768], P('tensor'), may hold values from -0.625 to 0.625
- output_bias: float32 [768], P('tensor'), may hold values from -1.5 to 1.5
- mlp_gain: float32 [768], replicated, may hold values from 0.5 to 1.5
- mlp_shift: float32 [768], replicated, may hold values from -1.5 to 1.5
- up_weight: bfloat16 [768, 3072], P(None, 'tensor'), may hold values from -0.21875 to 0.21875
- up_bias: float32 [3072], P('tensor'), may hold values from -2.5 to 2.5
- down_weight: bfloat16 [3072, 768], P('tensor'), may hold values from -0.15625 to 0.15625
- down_bias: float32 [768], P('tensor'), may hold values from -1.5 to 1.5
- cotangent: bfloat16 [24, 736, 768], P('dp', None, 'tensor'), may hold values from -6 to 6
Outputs:
- result: bfloat16 [24, 736, 768], P('dp', None, 'tensor')
- grad_tokens: bfloat16 [24, 736, 768], P('dp', None, 'tensor')
- grad_attn_gain: float32 [768], P('tensor')
- grad_attn_shift: float32 [768], P('tensor')
- grad_query_weight: float32 [768, 768], P(None, 'tensor')
- grad_key_weight: float32 [768, 768], P(None, 'tensor')
- grad_value_weight: float32 [768, 768], P(None, 'tensor')
- grad_query_bias: float32 [768], P('tensor')
- grad_value_bias: float32 [768], P('tensor')
- grad_output_weight: float32 [768, 768], P('tensor')
- grad_output_bias: float32 [768], P('tensor')
- grad_mlp_gain: float32 [768], P('tensor')
- grad_mlp_shift: float32 [768], P('tensor')
- grad_up_weight: float32 [768, 3072], P(None, 'tensor')
- grad_up_bias: float32 [3072], P('tensor')
- grad_down_weight: float32 [3072, 768], P('tensor')
- grad_down_bias: float32 [768], P('tensor')
Inputs may be any that keep to these rules, and one draw needn't show every extreme that they name: horizon[c] is the number of future frames of clip c; the clip's first 256 + 16 * horizon[c] rows are real, the rest of its 736 rows are padding.
All inputs are finite; a program needn't handle non-finite values.
Results may differ from a plain program's by a relative error of at most 0.012.
Values may be sent and summed in bfloat16 or wider, within the bound.
No kernel may reach another device: no remote copies, remote signals or barrier semaphores. Data moves between devices by JAX's collectives and lax.ppermute only.
A program may use at most 192 MiB of HBM per device.

v0:
```python
from functools import partial
import jax
import jax.numpy as jnp
from jax import lax
from jax.sharding import PartitionSpec as P

HDIM = 64
CONTEXT = 256
FRAME = 16
EPS = 1e-05
NEGATIVE = -1e30


def matmul(left, right):
    return jnp.dot(left, right, preferred_element_type=jnp.float32)


def inner_rows(left, right):
    return lax.dot_general(
        left, right, (((0,), (0,)), ((), ())), preferred_element_type=jnp.float32
    )


def times_transposed(left, right):
    return lax.dot_general(
        left, right, (((1,), (1,)), ((), ())), preferred_element_type=jnp.float32
    )


def normalize(rows):
    row_mean = jnp.mean(rows, axis=1, keepdims=True)
    centered = rows - row_mean
    row_var = jnp.mean(centered * centered, axis=1, keepdims=True)
    inv_std = lax.rsqrt(row_var + EPS)
    return (centered * inv_std, inv_std)


def clip_mask(clip_rows, length):
    position = jnp.arange(clip_rows, dtype=jnp.int32)
    return (position[None, :] <= position[:, None]) & (position[None, :] < length)


def clip_scores(query_clip, key_clip, length):
    factor = query_clip.shape[-1] ** (-0.5)
    scores = (
        jnp.einsum("qhd,khd->hqk", query_clip, key_clip, preferred_element_type=jnp.float32)
        * factor
    )
    allowed = clip_mask(query_clip.shape[0], length)
    return (jnp.where(allowed[None], scores, NEGATIVE), allowed, factor)


def attend_forward(pieces):
    query_clip, key_clip, value_clip, length = pieces
    scores, allowed, factor = clip_scores(query_clip, key_clip, length)
    row_max = jnp.max(scores, axis=2, keepdims=True)
    exp_terms = jnp.exp(scores - row_max)
    row_total = jnp.sum(exp_terms, axis=2, keepdims=True)
    attn_prob = (exp_terms / row_total).astype(jnp.bfloat16)
    mixed = jnp.einsum("hqk,khd->qhd", attn_prob, value_clip, preferred_element_type=jnp.float32)
    return (mixed.astype(jnp.bfloat16), (row_max + jnp.log(row_total))[:, :, 0])


def attend_backward(pieces):
    query_clip, key_clip, value_clip, grad_mixed, log_total, length = pieces
    scores, allowed, factor = clip_scores(query_clip, key_clip, length)
    attn_prob = jnp.where(allowed[None], jnp.exp(scores - log_total[:, :, None]), 0.0)
    grad_value = jnp.einsum(
        "hqk,qhd->khd",
        attn_prob.astype(jnp.bfloat16),
        grad_mixed,
        preferred_element_type=jnp.float32,
    ).astype(jnp.bfloat16)
    grad_prob = jnp.einsum(
        "qhd,khd->hqk", grad_mixed, value_clip, preferred_element_type=jnp.float32
    )
    row_delta = jnp.sum(attn_prob * grad_prob, axis=2, keepdims=True)
    grad_score = (attn_prob * (grad_prob - row_delta)).astype(jnp.bfloat16)
    grad_query = (
        jnp.einsum("hqk,khd->qhd", grad_score, key_clip, preferred_element_type=jnp.float32)
        * factor
    ).astype(jnp.bfloat16)
    grad_key = (
        jnp.einsum("hqk,qhd->khd", grad_score, query_clip, preferred_element_type=jnp.float32)
        * factor
    ).astype(jnp.bfloat16)
    return (grad_query, grad_key, grad_value)


def norm_back(grad_part, normed, inv_std, gain, own_start, own_width):
    grad_norm = lax.psum(grad_part, "tensor")
    scaled = grad_norm * gain
    first_mean = jnp.mean(scaled, axis=1, keepdims=True)
    second_mean = jnp.mean(scaled * normed, axis=1, keepdims=True)
    grad_full = inv_std * (scaled - first_mean - normed * second_mean)
    grad_in = lax.dynamic_slice_in_dim(grad_full, own_start, own_width, 1)
    grad_own = lax.dynamic_slice_in_dim(grad_norm, own_start, own_width, 1)
    normed_own = lax.dynamic_slice_in_dim(normed, own_start, own_width, 1)
    grad_gain = jnp.sum(grad_own * normed_own, axis=0)
    grad_shift = jnp.sum(grad_own, axis=0)
    return (grad_in, grad_gain, grad_shift)


def local(
    tokens,
    horizon,
    attn_gain,
    attn_shift,
    query_weight,
    key_weight,
    value_weight,
    query_bias,
    value_bias,
    output_weight,
    output_bias,
    mlp_gain,
    mlp_shift,
    up_weight,
    up_bias,
    down_weight,
    down_bias,
    cotangent,
):
    clip_count, clip_rows, own_width = tokens.shape
    row_count = clip_count * clip_rows
    own_start = lax.axis_index("tensor") * own_width
    lengths = CONTEXT + FRAME * horizon
    gathered = (
        lax.all_gather(tokens, "tensor", axis=2, tiled=True)
        .reshape(row_count, -1)
        .astype(jnp.float32)
    )
    normed_one, inv_one = normalize(gathered)
    acts_one = (normed_one * attn_gain + attn_shift).astype(jnp.bfloat16)
    queries = (matmul(acts_one, query_weight) + query_bias).astype(jnp.bfloat16)
    keys_all = matmul(acts_one, key_weight).astype(jnp.bfloat16)
    values = (matmul(acts_one, value_weight) + value_bias).astype(jnp.bfloat16)
    head_count = queries.shape[1] // HDIM
    shaped = (clip_count, clip_rows, head_count, HDIM)
    query_four = queries.reshape(shaped)
    key_four = keys_all.reshape(shaped)
    value_four = values.reshape(shaped)
    mixed, log_total = lax.map(attend_forward, (query_four, key_four, value_four, lengths))
    mixed = mixed.reshape(row_count, -1)
    attn_own = lax.psum_scatter(
        matmul(mixed, output_weight), "tensor", scatter_dimension=1, tiled=True
    )
    middle = tokens.reshape(row_count, own_width).astype(jnp.float32) + attn_own + output_bias
    middle_all = lax.all_gather(middle.astype(jnp.bfloat16), "tensor", axis=1, tiled=True).astype(
        jnp.float32
    )
    normed_two, inv_two = normalize(middle_all)
    acts_two = (normed_two * mlp_gain + mlp_shift).astype(jnp.bfloat16)
    hidden_pre = matmul(acts_two, up_weight) + up_bias
    hidden_full, gelu_back = jax.vjp(partial(jax.nn.gelu, approximate=True), hidden_pre)
    hidden = hidden_full.astype(jnp.bfloat16)
    mlp_own = lax.psum_scatter(
        matmul(hidden, down_weight).astype(jnp.bfloat16), "tensor", scatter_dimension=1, tiled=True
    ).astype(jnp.float32)
    result = (
        (middle + mlp_own + down_bias)
        .astype(jnp.bfloat16)
        .reshape(clip_count, clip_rows, own_width)
    )
    valid = (jnp.arange(clip_rows, dtype=jnp.int32)[None, :] < lengths[:, None]).astype(jnp.float32)
    grad_out = (cotangent.astype(jnp.float32) * valid[:, :, None]).reshape(row_count, own_width)
    grad_all = lax.all_gather(grad_out.astype(jnp.bfloat16), "tensor", axis=1, tiled=True)
    grad_down_bias = jnp.sum(grad_out, axis=0)
    grad_down_weight = inner_rows(hidden, grad_all)
    grad_hidden = times_transposed(grad_all, down_weight)
    grad_pre = gelu_back(grad_hidden)[0].astype(jnp.bfloat16)
    grad_up_bias = jnp.sum(grad_pre.astype(jnp.float32), axis=0)
    grad_up_weight = inner_rows(acts_two, grad_pre)
    back_two, grad_mlp_gain, grad_mlp_shift = norm_back(
        times_transposed(grad_pre, up_weight), normed_two, inv_two, mlp_gain, own_start, own_width
    )
    grad_middle = grad_out + back_two
    grad_mid_all = lax.all_gather(grad_middle.astype(jnp.bfloat16), "tensor", axis=1, tiled=True)
    grad_output_bias = jnp.sum(grad_middle, axis=0)
    grad_output_weight = inner_rows(mixed, grad_mid_all)
    grad_mixed = times_transposed(grad_mid_all, output_weight).astype(jnp.bfloat16)
    grad_query, grad_key, grad_value = lax.map(
        attend_backward,
        (query_four, key_four, value_four, grad_mixed.reshape(shaped), log_total, lengths),
    )
    grad_query = grad_query.reshape(row_count, -1)
    grad_key = grad_key.reshape(row_count, -1)
    grad_value = grad_value.reshape(row_count, -1)
    grad_query_bias = jnp.sum(grad_query.astype(jnp.float32), axis=0)
    grad_value_bias = jnp.sum(grad_value.astype(jnp.float32), axis=0)
    grad_query_weight = inner_rows(acts_one, grad_query)
    grad_key_weight = inner_rows(acts_one, grad_key)
    grad_value_weight = inner_rows(acts_one, grad_value)
    back_in = (
        times_transposed(grad_query, query_weight)
        + times_transposed(grad_key, key_weight)
        + times_transposed(grad_value, value_weight)
    )
    back_one, grad_attn_gain, grad_attn_shift = norm_back(
        back_in, normed_one, inv_one, attn_gain, own_start, own_width
    )
    grad_rows = (
        (grad_middle + back_one).astype(jnp.bfloat16).reshape(clip_count, clip_rows, own_width)
    )
    summed = lax.psum(
        (
            grad_attn_gain,
            grad_attn_shift,
            grad_query_weight,
            grad_key_weight,
            grad_value_weight,
            grad_query_bias,
            grad_value_bias,
            grad_output_weight,
            grad_output_bias,
            grad_mlp_gain,
            grad_mlp_shift,
            grad_up_weight,
            grad_up_bias,
            grad_down_weight,
            grad_down_bias,
        ),
        "dp",
    )
    return (result, grad_rows) + tuple(summed)


def solution(mesh):
    placed = (
        P("dp", None, "tensor"),
        P("dp"),
        P(),
        P(),
        P(None, "tensor"),
        P(None, "tensor"),
        P(None, "tensor"),
        P("tensor"),
        P("tensor"),
        P("tensor", None),
        P("tensor"),
        P(),
        P(),
        P(None, "tensor"),
        P("tensor"),
        P("tensor", None),
        P("tensor"),
        P("dp", None, "tensor"),
    )
    return jax.shard_map(
        local,
        mesh=mesh,
        in_specs=placed,
        out_specs=(
            P("dp", None, "tensor"),
            P("dp", None, "tensor"),
            P("tensor"),
            P("tensor"),
            P(None, "tensor"),
            P(None, "tensor"),
            P(None, "tensor"),
            P("tensor"),
            P("tensor"),
            P("tensor", None),
            P("tensor"),
            P("tensor"),
            P("tensor"),
            P(None, "tensor"),
            P("tensor"),
            P("tensor", None),
            P("tensor"),
        ),
        check_vma=False,
    )
```

profile of v0, /device:TPU:0, one launch (start us, length us, event | category | flops | bytes accessed | tf_op | source)
XLA Modules:
  0.0 904.3 jit_solution(11059979735407355032)
XLA Ops:
  8.7 34.4 %all-gather.5.cloned.1.call-done = bf16[3,736,768]{1,2,0:T(8,128)(2,1)} async-done(((bf16[3,736,192]{1,2,0:T(8,128)(2,1)}), bf16[3,736,768]{1,2,0:T(8,128)(2,1)}) %all-gather.5.cloned.1.call-update) | async-done | bytes 3391504 | tf_op jit(solution)/shard_map/all_gather | solution.py:129
  43.1 6.1 copy.136
  49.1 2.6 convert_reduce_fusion.2
  53.5 5.9 fusion.66
  63.8 4.1 fusion.68
  67.9 2.8 reshape.313
  71.7 3.2 fusion.69
  74.9 2.3 reshape.314
  79.6 25.4 %while.26 = (s32[]{:T(128)}, bf16[3,736,3,64]{1,3,2,0:T(8,128)(2,1)}, f32[3,3,736]{2,1,0:T(4,128)S(1)}, bf16[3,736,3,64]{1,3,2,0:T(8,128)(2,1)}, s32[3]{0:T(128)...) while((s32[]{:T(128)}, bf16[3,736,3,64]{1,3,2,0:T(8,128)(2,1)}, ...), condition=%wide.region_5.6_spmd, body=%wide.region_2.5_spmd.sunk | while | flops 436746816 | bytes 22955696 | solution.py:143
  84.0 4.0 fusion.156
  92.5 4.0 fusion.156
  101.0 4.0 fusion.156
  105.0 3.6 copy.140
  108.6 3.6 reshape.316
  112.2 5.1 convolution_bitcast_fusion
  118.5 2.2 copy.135
  120.7 3.4 reshape.324
  124.0 57.7 %reduce-scatter.7.cloned.1.call-done = f32[192,2208]{1,0:T(8,128)} async-done(((f32[768,2208]{1,0:T(8,128)}), f32[192,2208]{1,0:T(8,128)}) %reduce-scatter.7.cloned.1.call-update) | async-done | bytes 1695760
  181.7 2.6 fusion.81
  186.4 2.6 copy.146
  189.1 3.2 reshape.318
  193.3 21.9 %all-gather.7.cloned.1.call-done = bf16[2208,768]{0,1:T(8,128)(2,1)} async-done(((bf16[2208,192]{0,1:T(8,128)(2,1)}), bf16[2208,768]{0,1:T(8,128)(2,1)}) %all-gather.7.cloned.1.call-update) | async-done | bytes 3391504 | tf_op jit(solution)/shard_map/all_gather | solution.py:149
  215.2 5.7 copy.143
  220.9 2.6 convert_reduce_fusion
  225.3 5.5 fusion.79
  230.8 17.1 %all-gather.9.cloned.1.call-done = bf16[2208,768]{0,1:T(8,128)(2,1)} async-done(((bf16[2208,192]{0,1:T(8,128)(2,1)}), bf16[2208,768]{0,1:T(8,128)(2,1)}) %all-gather.9.cloned.1.call-update) | async-done | bytes 3391504 | tf_op jit(solution)/shard_map/all_gather | solution.py:167
  248.0 12.0 %convert_reduce_fusion.1 = (f32[768]{0:T(1024)}, bf16[2208,768]{1,0:T(8,128)(2,1)S(1)}, bf16[2208,768]{1,0:T(8,128)(2,1)}) fusion(f32[2208,768]{1,0:T(8,128)} %fusion.79, f32[768]{0:T(1024)S(1)} %copy-done.52, bf16[2208,768]{0,1:T(8,128)(2,1)} %all-gather.9.cloned.1.call-done, bf16[768,768]{1,0:T(8,128)(2,1)S(1)} %copy-done), kind=kOutput, calls=%fused_computation.80 | convolution fusion | flops 2647055616 | bytes 18143232 | tf_op jit(solution)/shard_map/dot_general | solution.py:25
  261.7 4.8 fusion.90
  268.5 125.8 %all-reduce.6.cloned.1.call-done = f32[2208,768]{1,0:T(8,128)} async-done(((f32[2208,768]{1,0:T(8,128)}), f32[2208,768]{1,0:T(8,128)}) %all-reduce.6.cloned.1.call-update) | async-done | bytes 6782992 | tf_op jit(solution)/shard_map/psum | solution.py:91
  394.2 6.3 fusion.86
  400.6 4.6 dynamic-slice_reduce_fusion
  406.2 2.3 copy.148
  408.6 15.8 %fusion.67 = bf16[768,2208]{1,0:T(8,128)(2,1)} fusion(bf16[2208,768]{1,0:T(8,128)(2,1)} %get-tuple-element.351, bf16[768,768]{1,0:T(8,128)(2,1)S(1)} %copy-done), kind=kOutput, calls=%fused_computation.92 | convolution fusion | flops 2606358528 | bytes 7962624 | tf_op jit(solution)/shard_map/dot_general | solution.py:15
  424.4 15.2 %all-gather.11.cloned.1.call-done = bf16[2208,768]{0,1:T(8,128)(2,1)} async-done(((bf16[2208,192]{0,1:T(8,128)(2,1)}), bf16[2208,768]{0,1:T(8,128)(2,1)}) %all-gather.11.cloned.1.call-update) | async-done | bytes 3391504 | tf_op jit(solution)/shard_map/all_gather | solution.py:178
  439.6 2.9 convolution_convert_fusion.1
  442.5 2.3 reshape.319
  449.1 46.8 %while.27 = (s32[]{:T(128)}, bf16[3,736,3,64]{1,3,2,0:T(8,128)(2,1)}, bf16[3,736,3,64]{1,3,2,0:T(8,128)(2,1)}, bf16[3,736,3,64]{1,3,2,0:T(8,128)(2,1)}, bf16[3,7...) while((s32[]{:T(128)}, ...), condition=%wide.region_15.16_spmd, body=%wide.region_13.15_spmd.sunk | while | flops 1058095680 | bytes 86495392 | solution.py:182
  450.7 2.2 fusion.165
  452.9 2.5 multiply_reduce_fusion.7
  455.7 4.0 multiply_convert_fusion.3
  466.2 2.2 fusion.165
  468.5 2.5 multiply_reduce_fusion.7
  471.2 4.1 multiply_convert_fusion.3
  481.8 2.2 fusion.165
  484.1 2.5 multiply_reduce_fusion.7
  486.8 4.0 multiply_convert_fusion.3
  495.9 2.9 copy.153
  498.8 2.6 reshape.320
  501.4 2.9 copy.155
  504.4 3.4 reshape.322
  507.8 2.9 copy.154
  510.7 3.6 reshape.321
  516.8 3.9 add_add_fusion
  521.4 3.0 add_convert_fusion
  524.5 6.9 fusion.94
  531.4 4.9 fusion.78
  544.9 3.6 add_convert_fusion.3
  548.4 3.8 reshape.317
  552.3 2.3 copy.157
  556.3 92.2 %all-reduce.8.cloned.1.call-done = f32[2208,768]{1,0:T(8,128)} async-done(((f32[2208,768]{1,0:T(8,128)}), f32[2208,768]{1,0:T(8,128)}) %all-reduce.8.cloned.1.call-update) | async-done | bytes 6782992 | tf_op jit(solution)/shard_map/psum | solution.py:91
  648.5 6.1 fusion.85
  654.6 4.8 dynamic-slice_reduce_fusion.1
  660.9 39.5 %all-reduce = (f32[192]{0:T(256)}, f32[192]{0:T(256)}, f32[192]{0:T(256)}, f32[192]{0:T(256)}, f32[192]{0:T(256)}, /*index=5*/f32[192]{0:T(256)}, f32[192]{0:T(256)}, f32[768]{0:T(1024)}, f32[192]{0:T(256)}) all-reduce(f32[192]{0:T(256)S(1)} %get-tuple-element.287, ...), channel_id=1, replica_groups=mesh['dp'=8,'tensor'=4] {'dp'}, use_global_device_ids=true, to_apply=%region_20.21 | all-reduce | flops 2304 | bytes 18432 | tf_op jit(solution)/shard_map/psum | solution.py:205
  700.3 187.3 %all-reduce.10.cloned.1.call-done = (f32[768,192]{0,1:T(8,128)}, f32[768,192]{0,1:T(8,128)}, f32[768,192]{0,1:T(8,128)}, f32[192,768]{1,0:T(8,128)}, f32[768,768]{1,0:T(8,128)}, /*index=5*/f32[768,768]{1,0:T(8,128)}) async-done(((f32[768,192]{0,1:T(8,128)}, f32[768,192]{0,1:T(8,128)}, f32[768,192]{0,1:T(8,128)}, f32[192,768]{1,0:T(8,128)}, f32[768,768]{1,0:T(8,128)}, /*index=5*/f32[768,768]{1,0:T(8,128)}), ...) | async-done | bytes 7077904 | tf_op jit(solution)/shard_map/psum | solution.py:205
  (233 shorter events, 84.6 us)
Async XLA Ops:
  7.2 240.8 %copy-start = (bf16[768,768]{1,0:T(8,128)(2,1)S(1)}, bf16[768,768]{1,0:T(8,128)(2,1)}, u32[]{:S(2)}) copy-start(bf16[768,768]{1,0:T(8,128)(2,1)} %param.37) | copy-start | bytes 3538948
  7.2 35.9 %all-gather.5.cloned.1.call-start = ((), (), s32[]{:S(2)}) async-start(), calls=%async_computation.2 | async-start | bytes 4423680 | tf_op jit(solution)/shard_map/all_gather | solution.py:129
  7.9 173.8 %reduce-scatter.7.cloned.1.call-start = ((), (), s32[]{:S(2)}) async-start(), calls=%async_computation.8 | async-start | bytes 8847360
  49.1 3.0 copy-start.3
  49.1 4.3 copy-start.39
  49.1 4.3 copy-start.41
  52.1 7.2 copy-start.32
  53.3 6.0 copy-start.34
  53.4 5.9 copy-start.36
  53.5 7.7 copy-start.28
  59.4 1.8 copy-start.20
  62.4 1.4 copy-start.30
  62.4 1.4 copy-start.55
  67.9 3.8 copy-start.26
  67.9 3.8 copy-start.56
  74.9 4.7 copy-start.38
  105.0 12.3 %copy-start.6 = (bf16[3,736,3,64]{1,3,2,0:T(8,128)(2,1)}, bf16[3,736,3,64]{1,3,2,0:T(8,128)(2,1)S(1)}, u32[]{:S(2)}) copy-start(bf16[3,736,3,64]{1,3,2,0:T(8,128)(2,1)S(1)} %get-tuple-element.572) | copy-start | bytes 2543620
  105.0 12.3 %copy-start.8 = (bf16[3,736,3,64]{1,3,2,0:T(8,128)(2,1)}, bf16[3,736,3,64]{1,3,2,0:T(8,128)(2,1)S(1)}, u32[]{:S(2)}) copy-start(bf16[3,736,3,64]{1,3,2,0:T(8,128)(2,1)S(1)} %get-tuple-element.573) | copy-start | bytes 2543620
  105.0 7.2 copy-start.23
  117.3 64.4 %copy-start.45 = (f32[192]{0:T(256)S(1)}, f32[192]{0:T(256)}, u32[]{:S(2)}) copy-start(f32[192]{0:T(256)} %param.32) | copy-start | bytes 2308
  117.4 97.8 %all-gather.7.cloned.1.call-start = ((), (), s32[]{:S(2)}) async-start(), calls=%async_computation.3 | async-start | bytes 4423680 | tf_op jit(solution)/shard_map/all_gather | solution.py:149
  124.0 62.4 %copy-start.10 = (f32[2208,192]{0,1:T(8,128)}, f32[2208,192]{0,1:T(8,128)S(1)}, u32[]{:S(2)}) copy-start(f32[2208,192]{0,1:T(8,128)S(1)} %reshape.324) | copy-start | bytes 5087236
  184.3 63.7 %all-gather.9.cloned.1.call-start = ((), (), s32[]{:S(2)}) async-start(), calls=%async_computation.4 | async-start | bytes 4423680 | tf_op jit(solution)/shard_map/all_gather | solution.py:167
  193.3 201.0 %all-reduce.6.cloned.1.call-start = ((), (), s32[]{:S(2)}) async-start(), calls=%async_computation.5 | async-start | bytes 13565952 | tf_op jit(solution)/shard_map/psum | solution.py:91
  220.9 3.2 copy-start.4
  220.9 4.4 copy-start.44
  220.9 4.4 copy-start.50
  220.9 4.4 copy-start.53
  225.3 22.7 %copy-start.52 = (f32[768]{0:T(1024)S(1)}, f32[768]{0:T(1024)}, u32[]{:S(2)}) copy-start(f32[768]{0:T(1024)} %param.36) | copy-start | bytes 9220
  248.0 13.7 %copy-start.51 = (bf16[768,768]{1,0:T(8,128)(2,1)S(1)}, bf16[768,768]{1,0:T(8,128)(2,1)}, u32[]{:S(2)}) copy-start(bf16[768,768]{1,0:T(8,128)(2,1)} %param.35) | copy-start | bytes 3538948
  260.0 1.7 copy-start.57
  266.5 173.1 %all-gather.11.cloned.1.call-start = ((), (), s32[]{:S(2)}) async-start(), calls=%async_computation.6 | async-start | bytes 4423680 | tf_op jit(solution)/shard_map/all_gather | solution.py:178
  394.2 6.3 copy-start.15
  408.5 135.7 %reduce-scatter.9.cloned.1.call-start = ((), (), s32[]{:S(2)}) async-start(), calls=%async_computation.9 | async-start | bytes 4423680
  424.4 15.3 %copy-start.24 = (bf16[192,768]{1,0:T(8,128)(2,1)S(1)}, bf16[192,768]{1,0:T(8,128)(2,1)}, u32[]{:S(2)}) copy-start(bf16[192,768]{1,0:T(8,128)(2,1)} %param.31) | copy-start | bytes 884740
  424.4 224.1 %all-reduce.8.cloned.1.call-start = ((), (), s32[]{:S(2)}) async-start(), calls=%async_computation.7 | async-start | bytes 13565952 | tf_op jit(solution)/shard_map/psum | solution.py:91
  450.6 2.2 copy-start.7
  450.7 2.2 copy-start.9
  452.9 2.7 copy-start.2
  466.2 2.2 copy-start.7
  466.2 2.2 copy-start.9
  468.4 2.7 copy-start.2
  481.8 2.2 copy-start.7
  481.8 2.2 copy-start.9
  484.1 2.7 copy-start.2
  504.3 10.0 %copy-start.27 = (bf16[768,192]{0,1:T(8,128)(2,1)S(1)}, bf16[768,192]{0,1:T(8,128)(2,1)}, u32[]{:S(2)}) copy-start(bf16[768,192]{0,1:T(8,128)(2,1)} %param.26) | copy-start | bytes 884740
  515.6 1.2 copy-start.31
  520.7 366.9 %all-reduce.10.cloned.1.call-start = ((), (), s32[]{:S(2)}) async-start(), calls=%async_computation.10 | async-start | bytes 14155776 | tf_op jit(solution)/shard_map/psum | solution.py:205
  521.4 3.0 copy-start.49
  524.4 6.9 copy-start.5
  524.5 6.9 copy-start.54
  524.5 6.9 copy-start.58
  531.4 4.9 copy-start.13
  536.2 1.7 copy-start.18
  539.6 2.2 copy-start.11
  539.6 2.4 copy-start.14
  544.2 10.4 %copy-start.16 = (bf16[3,736,3,64]{1,3,2,0:T(8,128)(2,1)S(1)}, bf16[3,736,3,64]{1,3,2,0:T(8,128)(2,1)}, u32[]{:S(2)}) copy-start(bf16[3,736,3,64]{1,3,2,0:T(8,128)(2,1)} %get-tuple-element.113) | copy-start | bytes 2543620
  648.5 6.1 copy-start.37
  654.6 6.2 copy-start.43
  654.6 6.2 copy-start.47
  887.6 6.1 copy-start.25
  887.6 6.9 copy-start.22
  891.6 4.3 copy-start.21
  894.5 2.8 copy-start.1
  (10 other events, 9.0 us)
Sparse Core Ops, SparseCore 0:
  9.6 33.4 all-gather.4
  117.5 64.1 reduce-scatter.6
  184.4 30.7 all-gather.6
  217.2 30.7 all-gather.8
  266.6 127.5 all-reduce.5
  408.7 30.9 all-gather.10
  442.2 40.3 reduce-scatter.8
  520.8 127.6 all-reduce.7
  654.7 232.8 all-reduce.9
where the time goes:
time: 915 us; the launch traced here: 904 us
  waiting for transfers between devices  552 us (60%)
  matrix products  125 us (14%)
  local copies, waits for them, and re-layouts  98.9 us (11%)
  other arithmetic  72.8 us (8%)
  blocking collectives  39.5 us (4%)
  between operations  14.9 us (2%)
    psum x2, waiting for transfers between devices, norm_back(): grad_norm = lax.psum(grad_part, 'tensor')  218 us
    psum x1, waiting for transfers between devices, local(): lax.psum((grad_attn_gain, grad_attn_shift, grad_query_weight, grad_key_we...  187 us
    unnamed x11, waiting for transfers between devices  58.5 us
    psum x1, blocking collectives, local(): lax.psum((grad_attn_gain, grad_attn_shift, grad_query_weight, grad_key_we...  39.5 us
    all_gather x1, waiting for transfers between devices, local(): lax.all_gather(tokens, 'tensor', axis=2, tiled=True).reshape(row_count, -1)  34.4 us
    dot_general x5, matrix products, matmul(): return jnp.dot(left, right, preferred_element_type=jnp.float32)  29.8 us
    dot_general x6, matrix products, times_transposed(): lax.dot_general(left, right, (((1,), (1,)), ((), ())), preferred_element_...  25.8 us
    all_gather x1, waiting for transfers between devices, local(): lax.all_gather(middle.astype(jnp.bfloat16), 'tensor', axis=1, tiled=True)  21.9 us
  transfers between devices with their start and end apart: 9, of which 8 were waited for; matrix products, arithmetic and copies ran while one was open for 19% of the time, Pallas kernels for 0%

commit v1 on v0

--- a/solution.py
+++ b/solution.py
@@ -88,7 +88,8 @@
 
 
 def norm_back(grad_part, normed, inv_std, gain, own_start, own_width):
-    grad_norm = lax.psum(grad_part, "tensor")
+    parts = lax.all_gather(grad_part, "tensor", axis=0, tiled=False)
+    grad_norm = parts.sum(axis=0)
     scaled = grad_norm * gain
     first_mean = jnp.mean(scaled, axis=1, keepdims=True)
     second_mean = jnp.mean(scaled * normed, axis=1, keepdims=True)

time: 915 us -> 1050 us (1.15)
  waiting for transfers between devices: 552 us -> 665 us
  other arithmetic: 72.8 us -> 93.9 us
  local copies, waits for them, and re-layouts: 98.9 us -> 111 us
    all_gather x0 -> x2, waiting for transfers between devices: none -> 309 us  [norm_back(): parts = lax.all_gather(grad_part, 'tensor', axis=0, tiled=False)]
    psum x2 -> x0, waiting for transfers between devices: 218 us -> none  [norm_back(): grad_norm = lax.psum(grad_part, 'tensor')]
    reduce_scatter x0 -> x2, waiting for transfers between devices: none -> 75.3 us  [the longest x1 56.5 us: local(): lax.psum_scatter(matmul(mixed, output_weight), 'tensor', scatter_dimensio...]
    unnamed x11 -> x9, waiting for transfers between devices: 58.5 us -> 0.81 us
    reduce_sum x0 -> x2, other arithmetic: none -> 26.7 us  [norm_back(): grad_norm = parts.sum(axis=0)]
    all_gather x1, waiting for transfers between devices: 15.2 us -> 30.8 us  [local(): lax.all_gather(grad_middle.astype(jnp.bfloat16), 'tensor', axis=1, tiled=...]
    reduce_sum x0 -> x2, local copies, waits for them, and re-layouts: none -> 15.4 us  [norm_back(): grad_norm = parts.sum(axis=0)]
    psum x1, waiting for transfers between devices: 187 us -> 173 us  [local(): lax.psum((grad_attn_gain, grad_attn_shift, grad_query_weight, grad_key_we...]
  transfers between devices with their start and end apart: 9 -> 9, of which waited for: 8 -> 9; matrix products, arithmetic and copies ran while one was open for 19% -> 10% of each run, Pallas kernels for 0% -> 0%
where the time goes in v1:
time: 1050 us; the launch traced here: 1040 us
  waiting for transfers between devices  665 us (63%)
  matrix products  117 us (11%)
  local copies, waits for them, and re-layouts  111 us (11%)
  other arithmetic  93.9 us (9%)
  blocking collectives  39.6 us (4%)
  between operations  14.9 us (1%)
    all_gather x2, waiting for transfers between devices, norm_back(): parts = lax.all_gather(grad_part, 'tensor', axis=0, tiled=False)  309 us
    psum x1, waiting for transfers between devices, local(): lax.psum((grad_attn_gain, grad_attn_shift, grad_query_weight, grad_key_we...  173 us
    reduce_scatter x1, waiting for transfers between devices, local(): lax.psum_scatter(matmul(mixed, output_weight), 'tensor', scatter_dimensio...  56.5 us
    psum x1, blocking collectives, local(): lax.psum((grad_attn_gain, grad_attn_shift, grad_query_weight, grad_key_we...  39.6 us
    all_gather x1, waiting for transfers between devices, local(): lax.all_gather(tokens, 'tensor', axis=2, tiled=True).reshape(row_count, -1)  34.4 us
    all_gather x1, waiting for transfers between devices, local(): lax.all_gather(grad_middle.astype(jnp.bfloat16), 'tensor', axis=1, tiled=...  30.8 us
    reduce_sum x2, other arithmetic, norm_back(): grad_norm = parts.sum(axis=0)  26.7 us
    dot_general x6, matrix products, times_transposed(): lax.dot_general(left, right, (((1,), (1,)), ((), ())), preferred_element_...  26 us
  transfers between devices with their start and end apart: 9, of which 9 were waited for; matrix products, arithmetic and copies ran while one was open for 10% of the time, Pallas kernels for 0%

profile of v1, /device:TPU:0, one launch (start us, length us, event | category | flops | bytes accessed | tf_op | source)
XLA Modules:
  0.0 1042.9 jit_solution(17749332798230605925)
XLA Ops:
  8.7 34.4 %all-gather.9.cloned.1.call-done = bf16[3,736,768]{1,2,0:T(8,128)(2,1)} async-done(((bf16[3,736,192]{1,2,0:T(8,128)(2,1)}), bf16[3,736,768]{1,2,0:T(8,128)(2,1)}) %all-gather.9.cloned.1.call-update) | async-done | bytes 3391504 | tf_op jit(solution)/shard_map/all_gather | solution.py:130
  43.1 6.0 copy.79
  49.1 2.6 convert_reduce_fusion.2
  53.4 5.9 copy.80
  59.4 5.7 add_convert_fusion.1
  69.9 2.9 convolution_convert_fusion.2
  72.9 2.3 reshape.336
  76.5 2.9 fusion.67
  79.4 2.3 reshape.335
  84.1 25.6 %while.26 = (s32[]{:T(128)}, bf16[3,736,3,64]{1,3,2,0:T(8,128)(2,1)}, f32[3,3,736]{2,1,0:T(4,128)S(1)}, bf16[3,736,3,64]{1,3,2,0:T(8,128)(2,1)}, s32[3]{0:T(128)...) while((s32[]{:T(128)}, bf16[3,736,3,64]{1,3,2,0:T(8,128)(2,1)}, ...), condition=%wide.region_5.6_spmd, body=%wide.region_2.5_spmd.sunk | while | flops 436746816 | bytes 22955696 | solution.py:144
  88.5 4.0 fusion.152
  97.0 4.0 fusion.152
  105.5 4.0 fusion.152
  109.7 3.3 copy.84
  113.0 3.4 reshape.337
  116.4 5.2 fusion.85
  124.9 4.5 reshape.345
  129.4 56.5 %reduce-scatter.3.cloned.1.call-done = f32[2208,192]{0,1:T(8,128)} async-done(((f32[2208,768]{0,1:T(8,128)}), f32[2208,192]{0,1:T(8,128)}) %reduce-scatter.3.cloned.1.call-update) | async-done | bytes 1695760 | tf_op jit(solution)/shard_map/reduce_scatter | solution.py:146
  185.9 3.1 fusion.76
  190.0 2.6 copy.85
  192.6 4.3 reshape.339
  196.9 2.9 convert_element_type.147
  199.9 20.0 %all-gather.11.cloned.1.call-done = bf16[2208,768]{0,1:T(8,128)(2,1)} async-done(((bf16[2208,192]{0,1:T(8,128)(2,1)}), bf16[2208,768]{0,1:T(8,128)(2,1)}) %all-gather.11.cloned.1.call-update) | async-done | bytes 3391504 | tf_op jit(solution)/shard_map/all_gather | solution.py:150
  220.0 2.7 convert_reduce_fusion
  224.0 6.2 fusion.79
  230.2 22.5 %all-gather.13.cloned.1.call-done = bf16[2208,768]{0,1:T(8,128)(2,1)} async-done(((bf16[2208,192]{0,1:T(8,128)(2,1)}), bf16[2208,768]{0,1:T(8,128)(2,1)}) %all-gather.13.cloned.1.call-update) | async-done | bytes 3391504 | tf_op jit(solution)/shard_map/all_gather | solution.py:168
  252.7 12.2 %convert_reduce_fusion.1 = (f32[768]{0:T(1024)}, bf16[2208,768]{1,0:T(8,128)(2,1)S(1)}, bf16[2208,768]{1,0:T(8,128)(2,1)}) fusion(f32[2208,768]{1,0:T(8,128)} %fusion.79, f32[768]{0:T(1024)S(1)} %copy-done.53, bf16[2208,768]{0,1:T(8,128)(2,1)} %all-gather.13.cloned.1.call-done, bf16[768,768]{1,0:T(8,128)(2,1)S(1)} %copy-done), kind=kOutput, calls=%fused_computation.82 | convolution fusion | flops 2647055616 | bytes 18143232 | tf_op jit(solution)/shard_map/dot_general | solution.py:25
  266.7 4.8 fusion.86
  271.6 165.8 %all-gather.17.cloned.1.call-done = f32[8832,768]{1,0:T(8,128)} async-done(((f32[2208,768]{1,0:T(8,128)}), f32[8832,768]{1,0:T(8,128)}) %all-gather.17.cloned.1.call-update) | async-done | bytes 27131920 | tf_op jit(solution)/shard_map/all_gather | solution.py:91
  437.3 12.9 %reduce_sum.199 = f32[2208,768]{1,0:T(8,128)} reduce(f32[4,2208,768]{2,1,0:T(8,128)} %bitcast.177, f32[]{:T(128)} %constant.71.clone.1), dimensions={0}, to_apply=%region_10.11 | reduce | flops 5087232 | bytes 33914884 | tf_op jit(solution)/shard_map/reduce_sum | solution.py:92
  450.3 7.7 copy.86
  458.0 5.2 fusion.80
  463.3 3.1 dynamic-slice_reduce_fusion
  468.6 30.8 %all-gather.15.cloned.1.call-done = bf16[2208,768]{0,1:T(8,128)(2,1)} async-done(((bf16[2208,192]{0,1:T(8,128)(2,1)}), bf16[2208,768]{0,1:T(8,128)(2,1)}) %all-gather.15.cloned.1.call-update) | async-done | bytes 3391504 | tf_op jit(solution)/shard_map/all_gather | solution.py:179
  499.4 2.9 convolution_convert_fusion.1
  502.3 2.5 reshape.340
  509.1 46.7 %while.27 = (s32[]{:T(128)}, bf16[3,736,3,64]{1,3,2,0:T(8,128)(2,1)}, bf16[3,736,3,64]{1,3,2,0:T(8,128)(2,1)}, bf16[3,736,3,64]{1,3,2,0:T(8,128)(2,1)}, bf16[3,7...) while((s32[]{:T(128)}, ...), condition=%wide.region_15.16_spmd, body=%wide.region_13.15_spmd.sunk | while | flops 1058095680 | bytes 83103872 | solution.py:183
  512.8 2.5 multiply_reduce_fusion.7
  515.6 4.0 multiply_convert_fusion.3
  528.4 2.5 multiply_reduce_fusion.7
  531.2 4.0 multiply_convert_fusion.3
  543.9 2.5 multiply_reduce_fusion.7
  546.7 4.0 multiply_convert_fusion.3
  555.9 3.0 copy.91
  558.9 2.6 reshape.341
  563.2 3.4 reshape.343
  566.7 2.9 copy.92
  569.6 2.8 reshape.342
  574.8 3.9 add_add_fusion
  578.8 6.4 convolution_convert_fusion
  585.3 9.4 fusion.90
  594.7 4.9 fusion.78
  601.7 142.8 %all-gather.19.cloned.1.call-done = f32[8832,768]{1,0:T(8,128)} async-done(((f32[2208,768]{1,0:T(8,128)}), f32[8832,768]{1,0:T(8,128)}) %all-gather.19.cloned.1.call-update) | async-done | bytes 27131920 | tf_op jit(solution)/shard_map/all_gather | solution.py:91
  744.5 13.8 %reduce_sum.202 = f32[2208,768]{1,0:T(8,128)} reduce(f32[4,2208,768]{2,1,0:T(8,128)} %bitcast.176, f32[]{:T(128)} %constant.71.clone.1), dimensions={0}, to_apply=%region_16.17 | reduce | flops 5087232 | bytes 33914884 | tf_op jit(solution)/shard_map/reduce_sum | solution.py:92
  758.3 5.3 add_convert_fusion.2
  768.7 18.8 %reduce-scatter.5.cloned.1.call-done = bf16[2208,192]{0,1:T(8,128)(2,1)} async-done(((bf16[2208,768]{0,1:T(8,128)(2,1)}), bf16[2208,192]{0,1:T(8,128)(2,1)}) %reduce-scatter.5.cloned.1.call-update) | async-done | bytes 847888 | tf_op jit(solution)/shard_map/reduce_scatter | solution.py:158
  787.5 3.1 add_convert_fusion.3
  790.5 3.7 reshape.338
  794.3 2.3 copy.97
  797.1 7.7 copy.94
  805.0 3.8 fusion.84
  808.8 2.7 dynamic-slice_reduce_fusion.1
  813.9 39.6 %all-reduce = (f32[192]{0:T(256)}, f32[192]{0:T(256)}, f32[192]{0:T(256)}, f32[192]{0:T(256)}, f32[192]{0:T(256)}, /*index=5*/f32[192]{0:T(256)}, f32[192]{0:T(256)}, f32[768]{0:T(1024)}, f32[192]{0:T(256)}) all-reduce(f32[192]{0:T(256)S(1)} %get-tuple-element.219, ...), channel_id=1, replica_groups=mesh['dp'=8,'tensor'=4] {'dp'}, use_global_device_ids=true, to_apply=%region_20.21 | all-reduce | flops 2304 | bytes 18432 | tf_op jit(solution)/shard_map/psum | solution.py:206
  853.5 172.8 %all-reduce.4.cloned.1.call-done = (f32[768,192]{0,1:T(8,128)}, f32[768,192]{0,1:T(8,128)}, f32[768,192]{0,1:T(8,128)}, f32[192,768]{1,0:T(8,128)}, f32[768,768]{1,0:T(8,128)}, /*index=5*/f32[768,768]{1,0:T(8,128)}) async-done(((f32[768,192]{0,1:T(8,128)}, f32[768,192]{0,1:T(8,128)}, f32[768,192]{0,1:T(8,128)}, f32[192,768]{1,0:T(8,128)}, f32[768,768]{1,0:T(8,128)}, /*index=5*/f32[768,768]{1,0:T(8,128)}), ...) | async-done | bytes 7077904 | tf_op jit(solution)/shard_map/psum | solution.py:206
  (235 shorter events, 90.4 us)
Async XLA Ops:
  7.2 245.5 %copy-start = (bf16[768,768]{1,0:T(8,128)(2,1)S(1)}, bf16[768,768]{1,0:T(8,128)(2,1)}, u32[]{:S(2)}) copy-start(bf16[768,768]{1,0:T(8,128)(2,1)} %param.37) | copy-start | bytes 3538948
  7.2 35.9 %all-gather.9.cloned.1.call-start = ((), (), s32[]{:S(2)}) async-start(), calls=%async_computation.2 | async-start | bytes 4423680 | tf_op jit(solution)/shard_map/all_gather | solution.py:130
  7.9 178.0 %reduce-scatter.3.cloned.1.call-start = ((), (), s32[]{:S(2)}) async-start(), calls=%async_computation.3 | async-start | bytes 8847360 | tf_op jit(solution)/shard_map/reduce_scatter | solution.py:146
  49.1 3.0 copy-start.2
  52.1 7.3 copy-start.31
  53.3 6.0 copy-start.35
  53.4 5.9 copy-start.33
  53.4 5.9 copy-start.38
  53.4 5.9 copy-start.40
  59.4 7.4 copy-start.29
  59.4 7.4 copy-start.56
  66.8 3.1 copy-start.23
  69.9 6.6 copy-start.27
  69.9 6.6 copy-start.57
  79.4 4.7 copy-start.37
  109.7 11.8 %copy-start.5 = (bf16[3,736,3,64]{1,3,2,0:T(8,128)(2,1)}, bf16[3,736,3,64]{1,3,2,0:T(8,128)(2,1)S(1)}, u32[]{:S(2)}) copy-start(bf16[3,736,3,64]{1,3,2,0:T(8,128)(2,1)S(1)} %get-tuple-element.509) | copy-start | bytes 2543620
  109.7 6.7 copy-start.22
  121.6 64.4 %copy-start.44 = (f32[192]{0:T(256)S(1)}, f32[192]{0:T(256)}, u32[]{:S(2)}) copy-start(f32[192]{0:T(256)} %param.32) | copy-start | bytes 2308
  121.6 98.4 %all-gather.11.cloned.1.call-start = ((), (), s32[]{:S(2)}) async-start(), calls=%async_computation.4 | async-start | bytes 4423680 | tf_op jit(solution)/shard_map/all_gather | solution.py:150
  129.4 59.8 %copy-start.25 = (bf16[3,736,192]{1,2,0:T(8,128)(2,1)S(1)}, bf16[3,736,192]{1,2,0:T(8,128)(2,1)}, u32[]{:S(2)}) copy-start(bf16[3,736,192]{1,2,0:T(8,128)(2,1)} %param.39) | copy-start | bytes 2543620
  189.1 63.7 %all-gather.13.cloned.1.call-start = ((), (), s32[]{:S(2)}) async-start(), calls=%async_computation.6 | async-start | bytes 4423680 | tf_op jit(solution)/shard_map/all_gather | solution.py:168
  199.8 24.1 %copy-start.43 = (f32[768]{0:T(1024)S(1)}, f32[768]{0:T(1024)}, u32[]{:S(2)}) copy-start(f32[768]{0:T(1024)} %param.33) | copy-start | bytes 9220
  199.9 24.1 %copy-start.54 = (f32[768]{0:T(1024)S(1)}, f32[768]{0:T(1024)}, u32[]{:S(2)}) copy-start(f32[768]{0:T(1024)} %param.34) | copy-start | bytes 9220
  199.9 237.5 %all-gather.17.cloned.1.call-start = ((), (), s32[]{:S(2)}) async-start(), calls=%async_computation.8 | async-start | bytes 33914880 | tf_op jit(solution)/shard_map/all_gather | solution.py:91
  220.0 3.1 copy-start.3
  220.0 4.1 copy-start.51
  224.0 28.7 %copy-start.53 = (f32[768]{0:T(1024)S(1)}, f32[768]{0:T(1024)}, u32[]{:S(2)}) copy-start(f32[768]{0:T(1024)} %param.36) | copy-start | bytes 9220
  252.7 14.0 %copy-start.52 = (bf16[768,768]{1,0:T(8,128)(2,1)S(1)}, bf16[768,768]{1,0:T(8,128)(2,1)}, u32[]{:S(2)}) copy-start(bf16[768,768]{1,0:T(8,128)(2,1)} %param.35) | copy-start | bytes 3538948
  271.5 227.9 %all-gather.15.cloned.1.call-start = ((), (), s32[]{:S(2)}) async-start(), calls=%async_computation.7 | async-start | bytes 4423680 | tf_op jit(solution)/shard_map/all_gather | solution.py:179
  458.0 5.3 copy-start.10
  468.6 276.0 %all-gather.19.cloned.1.call-start = ((), (), s32[]{:S(2)}) async-start(), calls=%async_computation.9 | async-start | bytes 33914880 | tf_op jit(solution)/shard_map/all_gather | solution.py:91
  510.6 2.2 copy-start.6
  512.8 2.8 copy-start.1
  526.2 2.2 copy-start.6
  528.4 2.8 copy-start.1
  543.9 2.8 copy-start.1
  555.9 5.6 copy-start.14
  563.2 9.2 copy-start.24
  578.7 208.8 %reduce-scatter.5.cloned.1.call-start = ((), (), s32[]{:S(2)}) async-start(), calls=%async_computation.5 | async-start | bytes 4423680 | tf_op jit(solution)/shard_map/reduce_scatter | solution.py:158
  585.2 9.5 copy-start.55
  585.2 441.1 %all-reduce.4.cloned.1.call-start = ((), (), s32[]{:S(2)}) async-start(), calls=%async_computation.10 | async-start | bytes 14155776 | tf_op jit(solution)/shard_map/psum | solution.py:206
  585.3 9.4 copy-start.4
  585.3 9.4 copy-start.59
  594.7 4.9 copy-start.11
  594.7 4.9 copy-start.13
  744.5 13.8 %copy-start.32 = (f32[3,736]{1,0:T(4,128)S(1)}, f32[3,736]{1,0:T(4,128)}, u32[]{:S(2)}) copy-start(f32[3,736]{1,0:T(4,128)} %copy-done.31) | copy-start | bytes 26500
  744.5 13.8 %copy-start.36 = (f32[3,736]{1,0:T(4,128)S(1)}, f32[3,736]{1,0:T(4,128)}, u32[]{:S(2)}) copy-start(f32[3,736]{1,0:T(4,128)} %copy-done.35) | copy-start | bytes 26500
  744.5 13.8 %copy-start.39 = (f32[768]{0:T(1024)S(1)}, f32[768]{0:T(1024)}, u32[]{:S(2)}) copy-start(f32[768]{0:T(1024)} %param.24) | copy-start | bytes 9220
  744.5 13.8 %copy-start.41 = (f32[768]{0:T(1024)S(1)}, f32[768]{0:T(1024)}, u32[]{:S(2)}) copy-start(f32[768]{0:T(1024)} %param.25) | copy-start | bytes 9220
  768.7 18.8 %copy-start.7 = (f32[2208,192]{0,1:T(8,128)S(1)}, f32[2208,192]{0,1:T(8,128)}, u32[]{:S(2)}) copy-start(f32[2208,192]{0,1:T(8,128)} %reshape.345) | copy-start | bytes 5087236
  768.7 18.8 %copy-start.45 = (f32[192]{0:T(256)S(1)}, f32[192]{0:T(256)}, u32[]{:S(2)}) copy-start(f32[192]{0:T(256)} %param.32) | copy-start | bytes 2308
  768.7 18.8 %copy-start.50 = (f32[192]{0:T(256)S(1)}, f32[192]{0:T(256)}, u32[]{:S(2)}) copy-start(f32[192]{0:T(256)} %param.38) | copy-start | bytes 2308
  790.5 6.0 copy-start.15
  790.5 6.3 copy-start.16
  805.0 3.8 copy-start.9
  805.0 3.9 copy-start.34
  811.5 2.3 copy-start.42
  811.6 2.3 copy-start.46
  811.6 2.3 copy-start.47
  811.6 2.3 copy-start.48
  811.6 2.3 copy-start.49
  1026.3 6.1 copy-start.26
  1026.3 6.9 copy-start.21
  1030.3 4.3 copy-start.20
  (9 other events, 13.3 us)
Sparse Core Ops, SparseCore 0:
  9.6 33.4 all-gather.8
  121.7 64.1 reduce-scatter.2
  189.2 30.7 all-gather.10
  221.9 30.7 all-gather.12
  271.6 165.6 all-gather.16
  468.7 30.7 all-gather.14
  578.8 165.6 all-gather.18
  747.1 40.3 reduce-scatter.4
  793.7 232.5 all-reduce.3
